TPU v7x, 32 devices: a whole 2x2x4 slice. The times are simulated.
32 devices in a mesh: prow: 4 (over y, x), pcol: 8 (over z, core).
Axes of the slice: x: 2, y: 2, z: 4, core: 2. Of those that a mesh axis runs over, the one named last changes fastest.
Arguments:
- inverse_block: bfloat16 [4096, 4096], P('prow', 'pcol'), as said below
- factor_cols: bfloat16 [4096, 2, 2048], P('prow', None, 'pcol'), may hold values from -6 to 6
- pattern: int32 [2, 32], replicated, may hold values from 0 to 1, as said below
Outputs:
- inverse_cols: bfloat16 [4096, 2, 2048], P(('pcol', 'prow'))
Inputs may be any that keep to these rules, and one draw needn't show every extreme that they name: inverse_block is symmetric up to rounding. `pattern`: for each supernode, each aligned group of 8 row blocks holds 1 to 4 nonzero blocks, and some group holds exactly 4.
All inputs are finite; a program needn't handle non-finite values.
Results may differ from a plain program's by a relative error of at most 0.013.
Values may be sent and summed in bfloat16 or wider, within the bound.
No kernel may reach another device: no remote copies, remote signals or barrier semaphores. Data moves between devices by JAX's collectives and lax.ppermute only.
A program may use at most 64 MiB of HBM per device.

v0:
```python
import jax
import jax.numpy as jnp
from jax import lax
from jax.sharding import PartitionSpec as P

MAXB = 4


def local(inverse_block, factor_cols, pattern):
    rows_here = inverse_block.shape[0]
    cols_here = inverse_block.shape[1]
    width_here = factor_cols.shape[2]
    groups = pattern.shape[1] // lax.axis_size("prow")
    block_rows = rows_here // groups
    own_mask = lax.dynamic_slice_in_dim(pattern, lax.axis_index("prow") * groups, groups, 1)
    slot_rank = jnp.cumsum(own_mask, axis=1) - 1
    slot_ids = jnp.arange(MAXB)
    onehot = (
        (slot_rank[None, :, :] == slot_ids[:, None, None]) & (own_mask[None, :, :] == 1)
    ).astype(jnp.bfloat16)
    blocks = factor_cols.reshape(groups, block_rows, 2, width_here)
    packed = jnp.einsum("ksb,brsw->krsw", onehot, blocks, preferred_element_type=jnp.float32)
    packed = packed.astype(jnp.bfloat16).reshape(MAXB * block_rows, 2, width_here)
    left_blocks = inverse_block.reshape(groups, block_rows, cols_here)
    packed_left = jnp.einsum(
        "ksb,brc->skrc", onehot, left_blocks, preferred_element_type=jnp.float32
    )
    packed_left = packed_left.astype(jnp.bfloat16).reshape(2, MAXB * block_rows, cols_here)
    gathered = lax.all_gather(packed, "pcol", axis=2, tiled=True)
    summed = lax.psum_scatter(
        jnp.einsum(
            "src,rsw->csw", packed_left, gathered, preferred_element_type=jnp.float32
        ).astype(jnp.bfloat16),
        "prow",
        scatter_dimension=0,
        tiled=True,
    ).astype(jnp.float32)
    return (-summed).astype(jnp.bfloat16)


def solution(mesh):
    return jax.shard_map(
        local,
        mesh=mesh,
        in_specs=(P("prow", "pcol"), P("prow", None, "pcol"), P()),
        out_specs=P(("pcol", "prow"), None, None),
        check_vma=False,
    )
```

profile of v0, /device:TPU:0, one launch (start us, length us, event | category | flops | bytes accessed | tf_op | source)
XLA Modules:
  0.0 135.1 jit_solution(13935510571011316371)
XLA Ops:
  6.5 0.0 copy-start
  6.5 0.0 copy-start.1
  6.5 0.0 all-gather.2.cloned.1.call-start
  6.5 0.9 broadcast_compare_fusion
  7.4 0.2 reduce_window_sum.11
  7.6 0.1 copy-done
  7.8 1.3 fusion.1
  9.1 0.1 copy.14
  9.1 1.0 copy.15
  10.1 0.0 all-gather.2.cloned.1.call-update
  10.2 0.0 reduce-scatter.4.cloned.1.call-start
  10.2 0.0 copy-done.1
  10.2 0.8 fusion
  11.1 0.2 copy.17
  11.3 48.6 %all-gather.2.cloned.1.call-done = bf16[512,2,2048]{0,2,1:T(8,128)(2,1)} async-done(((bf16[512,2,256]{0,2,1:T(8,128)(2,1)}), bf16[512,2,2048]{0,2,1:T(8,128)(2,1)}) %all-gather.2.cloned.1.call-update) | async-done | bytes 4194320 | tf_op jit(solution)/shard_map/all_gather | solution.py:29
  59.9 6.5 %convolution_convert_fusion = bf16[2,2048,512]{2,1,0:T(8,128)(2,1)} fusion(bf16[512,2,2048]{0,2,1:T(8,128)(2,1)} %all-gather.2.cloned.1.call-done, bf16[2,512,512]{2,1,0:T(8,128)(2,1)S(1)} %bitcast.29), kind=kOutput, calls=%fused_computation | convolution fusion | flops 2149580800 | bytes 9437184 | tf_op jit(solution)/shard_map/src,rsw->csw/dot_general | solution.py:31
  66.4 6.5 %copy.22 = bf16[512,4096]{1,0:T(8,128)(2,1)} copy(bf16[512,4096]{0,1:T(8,128)(2,1)} %bitcast.25) | data formatting | bytes 8388608
  72.8 0.0 reduce-scatter.4.cloned.1.call-update
  72.9 51.6 %reduce-scatter.4.cloned.1.call-done = bf16[128,4096]{1,0:T(8,128)(2,1)} async-done(((bf16[512,4096]{1,0:T(8,128)(2,1)}), bf16[128,4096]{1,0:T(8,128)(2,1)}) %reduce-scatter.4.cloned.1.call-update) | async-done | bytes 1048592
  124.4 1.6 %copy.23 = bf16[128,4096]{0,1:T(8,128)(2,1)S(1)} copy(bf16[128,4096]{1,0:T(8,128)(2,1)} %reduce-scatter.4.cloned.1.call-done) | data formatting | bytes 2097152
  126.0 0.2 negate_convert_fusion
  126.3 2.0 %copy.18 = bf16[128,2,2048]{2,1,0:T(2,128)(2,1)} copy(bf16[128,2,2048]{0,2,1:T(8,128)(2,1)S(1)} %negate_convert_fusion) | data formatting | bytes 2097152 | tf_op jit(solution)/shard_map/convert_element_type | solution.py:38
  (1 shorter events, 0.0 us)
Async XLA Ops:
  6.5 1.2 copy-start
  6.5 3.7 %copy-start.1 = (bf16[1024,512]{1,0:T(8,128)(2,1)S(1)}, bf16[1024,512]{1,0:T(8,128)(2,1)}, u32[]{:S(2)}) copy-start(bf16[1024,512]{1,0:T(8,128)(2,1)} %param.3) | copy-start | bytes 3145732
  6.5 53.4 %all-gather.2.cloned.1.call-start = ((), (), s32[]{:S(2)}) async-start(), calls=%async_computation.1 | async-start | bytes 4718592 | tf_op jit(solution)/shard_map/all_gather | solution.py:29
  10.2 114.3 %reduce-scatter.4.cloned.1.call-start = ((), (), s32[]{:S(2)}) async-start(), calls=%async_computation.2 | async-start | bytes 5242880
Sparse Core Ops, SparseCore 0:
  10.3 49.5 all-gather.1
  73.0 51.3 reduce-scatter.3
where the time goes:
time: 135 us
  waiting for transfers between devices  100 us (74%)
  between operations  13.4 us (10%)
  local copies, waits for them, and re-layouts  11.5 us (9%)
  matrix products  8.6 us (6%)
    unnamed x3, waiting for transfers between devices  51.6 us
    all_gather x1, waiting for transfers between devices, local(): gathered = lax.all_gather(packed, 'pcol', axis=2, tiled=True)  48.6 us
    unnamed x6, local copies, waits for them, and re-layouts  8.22 us
    dot_general x1, matrix products, local(): jnp.einsum('src,rsw->csw', packed_left, gathered, preferred_element_type=...  6.48 us
  transfers between devices with their start and end apart: 2, of which 2 were waited for; matrix products, arithmetic and copies ran while one was open for 1% of the time, Pallas kernels for 0%

commit v1 on v0

--- a/solution.py
+++ b/solution.py
@@ -4,6 +4,18 @@
 from jax.sharding import PartitionSpec as P
 
 MAXB = 4
+
+
+def collect(x, axis, dim):
+    ways, here, step = (lax.axis_size(axis), lax.axis_index(axis), x.shape[dim])
+    line, have = (x, 1)
+    while have < ways:
+        line = jnp.concatenate(
+            [line, lax.ppermute(line, axis, [(d, (d - have) % ways) for d in range(ways)])],
+            axis=dim,
+        )
+        have = 2 * have
+    return jnp.roll(line, here * step, axis=dim)
 
 
 def local(inverse_block, factor_cols, pattern):
@@ -26,7 +38,7 @@
         "ksb,brc->skrc", onehot, left_blocks, preferred_element_type=jnp.float32
     )
     packed_left = packed_left.astype(jnp.bfloat16).reshape(2, MAXB * block_rows, cols_here)
-    gathered = lax.all_gather(packed, "pcol", axis=2, tiled=True)
+    gathered = collect(packed, "pcol", 2)
     summed = lax.psum_scatter(
         jnp.einsum(
             "src,rsw->csw", packed_left, gathered, preferred_element_type=jnp.float32

time: 135 us -> 217 us (1.61)
  waiting for transfers between devices: 100 us -> 173 us
  starting transfers between devices: 0.04 us -> 5.19 us
  local copies, waits for them, and re-layouts: 11.5 us -> 15.4 us
    ppermute x0 -> x3, waiting for transfers between devices: none -> 121 us  [collect(): lax.ppermute(line, axis, [(d, (d - have) % ways) for d in range(ways)])]
    all_gather x1 -> x0, waiting for transfers between devices: 48.6 us -> none  [local(): gathered = lax.all_gather(packed, 'pcol', axis=2, tiled=True)]
    ppermute x0 -> x3, starting transfers between devices: none -> 5.19 us  [collect(): lax.ppermute(line, axis, [(d, (d - have) % ways) for d in range(ways)])]
    unnamed x6 -> x13, local copies, waits for them, and re-layouts: 8.22 us -> 10.2 us
    unnamed x3 -> x2, waiting for transfers between devices: 51.6 us -> 52 us
  transfers between devices with their start and end apart: 2 -> 4, of which waited for: 2 -> 4; matrix products, arithmetic and copies ran while one was open for 1% -> 2% of each run, Pallas kernels for 0% -> 0%
where the time goes in v1:
time: 217 us
  waiting for transfers between devices  173 us (80%)
  local copies, waits for them, and re-layouts  15.4 us (7%)
  between operations  13.5 us (6%)
  matrix products  7.68 us (4%)
  starting transfers between devices  5.19 us (2%)
  other arithmetic  2.77 us (1%)
    ppermute x3, waiting for transfers between devices, collect(): lax.ppermute(line, axis, [(d, (d - have) % ways) for d in range(ways)])  121 us
    unnamed x2, waiting for transfers between devices  52 us
    unnamed x13, local copies, waits for them, and re-layouts  10.2 us
    ppermute x3, starting transfers between devices, collect(): lax.ppermute(line, axis, [(d, (d - have) % ways) for d in range(ways)])  5.19 us
  transfers between devices with their start and end apart: 4, of which 4 were waited for; matrix products, arithmetic and copies ran while one was open for 2% of the time, Pallas kernels for 0%

profile of v1, /device:TPU:0, one launch (start us, length us, event | category | flops | bytes accessed | tf_op | source)
XLA Modules:
  0.0 217.1 jit_solution(7077341009677308527)
XLA Ops:
  6.5 0.0 copy-start
  6.5 0.0 reduce-scatter.4.cloned.1.call-start
  6.5 0.8 broadcast_compare_fusion
  7.4 0.2 reduce_window_sum.11
  7.6 0.2 copy-done
  7.8 1.3 fusion.6
  9.1 0.1 copy.18
  9.1 0.2 copy.22
  9.4 4.6 %collective-permute-start = (bf16[512,2,256]{0,2,1:T(8,128)(2,1)S(1)}, bf16[512,2,256]{0,2,1:T(8,128)(2,1)S(1)}, u32[]{:S(2)}, u32[]{:S(2)}) collective-permute-start(bf16[512,2,256]{0,2,1:T(8,128)(2,1)S(1)} %copy.22), channel_id=1, source_target_pairs={{0,7},{1,0},{2,1},{3,2},{4,3},{5,4},{6,5},{7,6},{8,15},{9,8},{10,9... | collective-permute-start | bytes 1572872 | tf_op jit(solution)/shard_map/ppermute | solution.py:14
  13.9 6.7 %collective-permute-done = bf16[512,2,256]{0,2,1:T(8,128)(2,1)S(1)} collective-permute-done((bf16[512,2,256]{0,2,1:T(8,128)(2,1)S(1)}, bf16[512,2,256]{0,2,1:T(8,128)(2,1)S(1)}, u32[]{:S(2)}, u32[]{:S(2)}) %collective-permute-start) | collective-permute-done | bytes 524320 | tf_op jit(solution)/shard_map/ppermute | solution.py:14
  20.6 0.1 pad_maximum_fusion.1
  20.7 0.6 collective-permute-start.1
  21.3 23.3 %collective-permute-done.1 = bf16[512,2,512]{0,2,1:T(8,128)(2,1)S(1)} collective-permute-done((bf16[512,2,512]{0,2,1:T(8,128)(2,1)S(1)}, bf16[512,2,512]{0,2,1:T(8,128)(2,1)S(1)}, u32[]{:S(2)}, u32[]{:S(2)}) %collective-permute-start.1) | collective-permute-done | bytes 1048608 | tf_op jit(solution)/shard_map/ppermute | solution.py:14
  44.6 1.5 pad_maximum_fusion
  46.1 0.0 collective-permute-start.2
  46.1 2.1 fusion.5
  48.2 1.2 copy.25
  49.3 0.0 copy-start.1
  49.4 0.1 constant_dynamic-update-slice_fusion.5
  49.5 90.5 %collective-permute-done.2 = bf16[512,2,1024]{0,2,1:T(8,128)(2,1)} collective-permute-done((bf16[512,2,1024]{0,2,1:T(8,128)(2,1)}, bf16[512,2,1024]{0,2,1:T(8,128)(2,1)}, u32[]{:S(2)}, u32[]{:S(2)}) %collective-permute-start.2) | collective-permute-done | bytes 2097184 | tf_op jit(solution)/shard_map/ppermute | solution.py:14
  140.0 1.7 constant_dynamic-update-slice_fusion.4
  141.8 0.1 constant_dynamic-update-slice_fusion.1
  141.9 1.7 constant_dynamic-update-slice_fusion
  143.6 0.0 copy-done.1
  143.6 4.3 %fusion.2 = bf16[2,2048,512]{2,1,0:T(8,128)(2,1)} fusion(bf16[2,512,512]{2,1,0:T(8,128)(2,1)S(1)} %bitcast.28, bf16[512,2,4096]{0,2,1:T(8,128)(2,1)S(1)} %constant_dynamic-update-slice_fusion, s32[]{:T(128)S(6)} %select_n.18), kind=kOutput, calls=%fused_computation.2 | convolution fusion | flops 2149580800 | bytes 9437188 | tf_op jit(solution)/shard_map/src,rsw->csw/dot_general | solution.py:43
  148.0 6.4 %copy.30 = bf16[512,4096]{1,0:T(8,128)(2,1)} copy(bf16[512,4096]{0,1:T(8,128)(2,1)} %bitcast.24) | data formatting | bytes 8388608
  154.4 0.0 reduce-scatter.4.cloned.1.call-update
  154.4 52.0 %reduce-scatter.4.cloned.1.call-done = bf16[128,4096]{1,0:T(8,128)(2,1)} async-done(((bf16[512,4096]{1,0:T(8,128)(2,1)}), bf16[128,4096]{1,0:T(8,128)(2,1)}) %reduce-scatter.4.cloned.1.call-update) | async-done | bytes 1048592
  206.4 1.6 copy.31
  208.0 0.2 negate_convert_fusion
  208.2 2.0 copy.26
  (5 shorter events, 0.1 us)
Async XLA Ops:
  6.5 1.2 copy-start
  6.5 199.8 %reduce-scatter.4.cloned.1.call-start = ((), (), s32[]{:S(2)}) async-start(), calls=%async_computation.1 | async-start | bytes 5242880
  9.4 11.3 %collective-permute-start = (bf16[512,2,256]{0,2,1:T(8,128)(2,1)S(1)}, bf16[512,2,256]{0,2,1:T(8,128)(2,1)S(1)}, u32[]{:S(2)}, u32[]{:S(2)}) collective-permute-start(bf16[512,2,256]{0,2,1:T(8,128)(2,1)S(1)} %copy.22), channel_id=1, source_target_pairs={{0,7},{1,0},{2,1},{3,2},{4,3},{5,4},{6,5},{7,6},{8,15},{9,8},{10,9... | collective-permute-start | bytes 1572872 | tf_op jit(solution)/shard_map/ppermute | solution.py:14
  20.7 23.9 %collective-permute-start.1 = (bf16[512,2,512]{0,2,1:T(8,128)(2,1)S(1)}, bf16[512,2,512]{0,2,1:T(8,128)(2,1)S(1)}, u32[]{:S(2)}, u32[]{:S(2)}) collective-permute-start(bf16[512,2,512]{0,2,1:T(8,128)(2,1)S(1)} %pad_maximum_fusion.1), channel_id=1, source_target_pairs={{0,6},{1,7},{2,0},{3,1},{4,2},{5,3},{6,4},{7,5},{8,14},{9,15},{10,... | collective-permute-start | bytes 3145736 | tf_op jit(solution)/shard_map/ppermute | solution.py:14
  46.1 93.9 %collective-permute-start.2 = (bf16[512,2,1024]{0,2,1:T(8,128)(2,1)}, bf16[512,2,1024]{0,2,1:T(8,128)(2,1)}, u32[]{:S(2)}, u32[]{:S(2)}) collective-permute-start(bf16[512,2,1024]{0,2,1:T(8,128)(2,1)} %pad_maximum_fusion), channel_id=1, source_target_pairs={{0,4},{1,5},{2,6},{3,7},{4,0},{5,1},{6,2},{7,3},{8,12},{9,13},{10,... | collective-permute-start | bytes 6291464 | tf_op jit(solution)/shard_map/ppermute | solution.py:14
  49.3 94.3 %copy-start.1 = (bf16[2,4,128,512]{3,2,1,0:T(8,128)(2,1)S(1)}, bf16[2,4,128,512]{3,2,1,0:T(8,128)(2,1)}, u32[]{:S(2)}) copy-start(bf16[2,4,128,512]{3,2,1,0:T(8,128)(2,1)} %copy.25) | copy-start | bytes 3145732
Sparse Core Ops, SparseCore 0:
  154.5 51.8 reduce-scatter.3
